TPU v7x, 128 devices: a whole 4x4x4 slice. The times are simulated.
128 devices in a mesh: grp: 8 (over y, core), tok: 16 (over x, z).
Axes of the slice: x: 4, y: 4, z: 4, core: 2. Of those that a mesh axis runs over, the one named last changes fastest.
Arguments:
- tokens: bfloat16 [8, 2048, 1280], P('grp', 'tok'), may hold values from -6 to 6
- seg_lengths: int32 [8, 32], P('grp'), may hold values from 1 to 256, 2048 in all within a row
- prefix_keys: bfloat16 [8, 4096, 1280], P('grp', 'tok'), may hold values from -6 to 6
- prefix_values: bfloat16 [8, 4096, 1280], P('grp', 'tok'), may hold values from -0.4375 to 0.4375
- w_qkv: bfloat16 [1280, 3840], replicated, may hold values from -0.15625 to 0.15625
- w_out: bfloat16 [1280, 1280], replicated, may hold values from -0.15625 to 0.15625
- qk_scale: float32 [1280], replicated, may hold values from 0.3 to 10
- attn_rate: float32 [1280], replicated, may hold values from 0.05 to 0.5
- w_up: bfloat16 [1280, 5120], P(None, 'grp'), may hold values from -0.15625 to 0.15625
- w_gate: bfloat16 [1280, 5120], P(None, 'grp'), may hold values from -0.15625 to 0.15625
- w_down: bfloat16 [5120, 1280], P('grp'), may hold values from -0.078125 to 0.078125
- up_scale: float32 [5120], P('grp'), may hold values from 0.5 to 2
- gate_scale: float32 [5120], P('grp'), may hold values from 0.5 to 2
- mlp_rate: float32 [1280], replicated, may hold values from 0.05 to 0.5
Outputs:
- mixed: bfloat16 [8, 2048, 1280], P('grp', 'tok')
Inputs may be any that keep to these rules, and one draw needn't show every extreme that they name: `seg_lengths`: row g lists the lengths of group g's 32 requests in order of position; they sum to 2048 and the longest is exactly 256.
All inputs are finite; a program needn't handle non-finite values.
Results may differ from a plain program's by a relative error of at most 0.0085.
The roundings to bfloat16 on the way count: a program that leaves them out, or rounds other values in their place, can miss the bound.
Values may be sent and summed in bfloat16 or wider, within the bound.
A program may use at most 128 MiB of HBM per device.

v0:
```python
import functools
import math

import jax
import jax.numpy as jnp
from jax import lax
from jax.experimental import pallas as pl
from jax.experimental.pallas import tpu as pltpu
from jax.sharding import PartitionSpec as P

D = 1280
HEAD = 64
LOCAL_HEADS = 5
HROWS = 320
ROWS = 128
PREF = 256
REQS = 32
EPS = 1e-06
MESH = pl.DeviceIdType.MESH
F32 = jnp.float32
BF16 = jnp.bfloat16


def unit(vector):
    return vector * lax.rsqrt(jnp.sum(vector * vector, axis=-1, keepdims=True) + EPS)


def head_unit(cols, scale):
    per_head = cols.reshape(2, HEAD, cols.shape[1])
    norm = lax.rsqrt(jnp.sum(per_head * per_head, axis=1, keepdims=True) + EPS)
    return (per_head * norm).reshape(cols.shape) * scale


def layer_kernel(
    lengths_ref, tok_ref, pk_ref, pv_ref, wqkv_hbm, wout_hbm, scale_ref, arate_ref, wup_hbm, wgate_hbm, wdown_hbm,
    uscale_ref, gscale_ref, mrate_ref, out_ref,
    wqkv, wout, wup, wgate, wdown, scale_t,
    key_s, val_s, q_s, sk_s, kx, vx, qx, sx, qz, kt, skt, starts, mask, sbuf, kloc, vloc, part, stat, ret, rstat, merged, att, mix_t,
    hid, blocks, give, take, total, send_y, recv_y, w_sem, sem,
):
    tok, grp = lax.axis_index("tok"), lax.axis_index("grp")
    x, z = tok // 4, tok % 4
    y, c = grp // 2, grp % 2

    def at_x(i):
        return {"tok": ((x + i) % 4) * 4 + z}

    def at_z(i):
        return {"tok": x * 4 + (z + i) % 4}

    def at_y(i):
        return {"grp": ((y + i) % 4) * 2 + c}

    partner = {"grp": y * 2 + (1 - c)}
    used = [0]
    arrivals = {}
    sends = []

    def send(name, src, dst, dev):
        n = used[0]
        used[0] += 2
        copy = pltpu.make_async_remote_copy(
            src_ref=src, dst_ref=dst, send_sem=sem.at[n], recv_sem=sem.at[n + 1], device_id=dev, device_id_type=MESH
        )
        copy.start()
        sends.append(copy)
        assert name not in arrivals
        arrivals[name] = (dst, n)

    def arrive(name):
        dst, n = arrivals[name]
        pltpu.make_async_remote_copy(
            src_ref=dst, dst_ref=dst, send_sem=sem.at[n], recv_sem=sem.at[n + 1], device_id=partner,
            device_id_type=MESH,
        ).wait_recv()

    barrier = pltpu.get_barrier_semaphore()
    for i in (1, 2, 3):
        for dev in (at_x(i), at_z(i), at_y(i)):
            pl.semaphore_signal(barrier, inc=1, device_id=dev, device_id_type=MESH)
    pl.semaphore_signal(barrier, inc=1, device_id=partner, device_id_type=MESH)

    loads = []

    def load(src, dst):
        copy = pltpu.make_async_copy(src, dst, w_sem.at[len(loads)])
        copy.start()
        loads.append(copy)

    for n in range(3):
        cols = pl.ds(n * D, D)
        load(wqkv_hbm.at[:, cols], wqkv.at[:, cols])
    load(wout_hbm, wout)
    load(wup_hbm, wup)
    load(wgate_hbm, wgate)
    load(wdown_hbm, wdown)

    for b in range(10):
        lanes = pl.ds(b * 128, 128)
        scale_t[lanes, :] = jnp.broadcast_to(scale_ref[:, lanes], (128, 128)).T
    for b in range(10):
        lanes = pl.ds(b * 128, 128)
        scale = scale_t[lanes, :]
        cols = pk_ref[:, lanes].astype(F32).T
        key_s[lanes, :] = head_unit(cols, jnp.concatenate([scale, scale], axis=1)).astype(BF16)
    pl.semaphore_wait(barrier, 10)

    def rows_of(ref, i):
        return ref.at[pl.ds(((x + i) % 4) * HROWS, HROWS), :]

    for i in (2, 1, 3):
        send(("k", 4 - i), rows_of(key_s, i), kx.at[4 - i], at_x(i))

    for b in range(10):
        lanes = pl.ds(b * 128, 128)
        val_s[lanes, :] = pv_ref[:, lanes].T

    hidden = unit(tok_ref[...].astype(F32))
    hid[...] = hidden
    hidden = hidden.astype(BF16)

    def project(n, b):
        cols = jnp.dot(hidden, wqkv[:, n * D + b * 256 : n * D + b * 256 + 256], preferred_element_type=F32)
        return [cols[:, a * 128 : a * 128 + 128].T for a in (0, 1)]

    loads[0].wait()
    for b in range(5):
        for a, cols in enumerate(project(0, b)):
            lanes = pl.ds(b * 256 + a * 128, 128)
            query = head_unit(cols, scale_t[lanes, :]).astype(BF16)
            q_s[lanes, :] = query * BF16(math.sqrt(HEAD))
    for i in (2, 1, 3):
        send(("q", 4 - i), rows_of(q_s, i), qx.at[4 - i], at_x(i))
    qx[0] = q_s[pl.ds(pl.multiple_of(x * HROWS, HROWS), HROWS), :]

    def forward_q(j):
        for e in (2, 1, 3):
            send(("qz", 4 - e, j), qx.at[j], qz.at[(4 - e) - 1, j], at_z(e))

    forward_q(0)
    for i in (2, 1, 3):
        send(("v", 4 - i), rows_of(val_s, i), vx.at[4 - i], at_x(i))
    for n in (1, 2):
        loads[n].wait()
        for b in range(5):
            for a, cols in enumerate(project(n, b)):
                lanes = pl.ds(b * 256 + a * 128, 128)
                if n == 1:
                    cols = head_unit(cols, scale_t[lanes, :])
                sk_s[n - 1, lanes, :] = cols.astype(BF16)
    for i in (2, 1, 3):
        src = sk_s.at[:, pl.ds(((x + i) % 4) * HROWS, HROWS), :]
        send(("s", 4 - i), src, sx.at[4 - i], at_x(i))
    own = pl.ds(pl.multiple_of(x * HROWS, HROWS), HROWS)
    kx[0] = key_s[own, :]
    vx[0] = val_s[own, :]
    sx[0] = sk_s[:, own, :]

    position = (
        lax.broadcasted_iota(jnp.int32, (16, ROWS), 0) * ROWS + lax.broadcasted_iota(jnp.int32, (16, ROWS), 1)
    )
    end = jnp.int32(0)
    first = jnp.zeros((16, ROWS), jnp.int32)
    for r in range(REQS):
        end = end + lengths_ref[0, r]
        first = jnp.where(position >= end, end, first)
    for t in range(16):
        starts[t] = jnp.broadcast_to(first[t : t + 1, :], (8, ROWS))
    for e in range(3):
        for j in range(4):
            tq = ((x + j) % 4) * 4 + (z + e) % 4
            kpos = (tq - e) * ROWS + lax.broadcasted_iota(jnp.int32, (ROWS, ROWS), 0)
            qpos = tq * ROWS + lax.broadcasted_iota(jnp.int32, (ROWS, ROWS), 1)
            allowed = (kpos >= starts[tq, pl.ds(0, 1), :]) & (kpos <= qpos)
            bias = jnp.where(allowed, 0.0, -1e30)
            apart = jnp.full((ROWS, ROWS), -1e30, F32)
            mask[e, j // 2, pl.ds((j % 2) * ROWS, ROWS), :] = jnp.concatenate(
                [apart, bias] if j % 2 else [bias, apart], axis=1
            )
    for d in range(4):
        for j in range(4):
            stat[d, j] = jnp.zeros((8, ROWS), F32)

    def turn_keys(j):
        for h in range(LOCAL_HEADS):
            kt[h, pl.ds(j * PREF, PREF), :] = kx[j, pl.ds(h * HEAD, HEAD), :].T

    turn_keys(0)
    for j in (1, 3, 2):
        arrive(("k", j))
        turn_keys(j)
    for j in (1, 3, 2):
        arrive(("q", j))
        forward_q(j)
    for j in (1, 3, 2):
        arrive(("v", j))

    def fold(v):
        return v.reshape(v.shape[0] // 8, 8, v.shape[1])

    def attend(e):
        local = e < 3

        def head_rows(h):
            return pl.ds(pl.multiple_of(h * HEAD, HEAD), HEAD)

        def score(h, n, j, high):
            j0, rows = 2 * n, head_rows(h)
            q = [qx[j0 + a, rows, :] if e == 0 else qz[e - 1, j0 + a, rows, :] for a in (0, 1)]
            keys = kt[h, pl.ds(j * PREF, PREF), :] if j < 4 else kloc[e, n, h]
            s = jnp.dot(keys, jnp.concatenate(q, axis=1), preferred_element_type=F32)
            if j == 4:
                s = s + mask[e, n]
            sbuf[n, pl.ds(j * PREF, PREF), :] = s
            top = jnp.max(fold(s), axis=0)
            return top if high is None else jnp.maximum(high, top)

        def blend(h, n, j, m, added, o):
            rows = head_rows(h)
            p = jnp.exp(sbuf[n, pl.ds(j * PREF, PREF), :] - m)
            more = jnp.sum(fold(p), axis=0)
            values = vx[j, rows, :] if j < 4 else vloc[e, n, rows, :]
            t = jnp.dot(values, p.astype(BF16), preferred_element_type=F32)
            return (more, t) if o is None else (added + more, o + t)

        parts = 5 if local else 4

        def step(h, n, high, after):
            m = jnp.max(high, axis=0, keepdims=True)
            high, added, o = None, None, None
            for j in range(parts):
                high = score(after, 1 - n, j, high)
                added, o = blend(h, n, j, m, added, o)
            added = jnp.sum(added, axis=0, keepdims=True)
            o = (o * (1.0 / added)).astype(BF16)
            lse = m + jnp.log(added)
            for a in (0, 1):
                lanes = slice(a * ROWS, (a + 1) * ROWS)
                part[e, 2 * n + a, head_rows(h), :] = o[:, lanes]
                stat[e, 2 * n + a, pl.ds(h, 1), :] = lse[:, lanes]
            return high

        def both_tiles(h, high):
            high = step(h, 0, high, h)
            return step(h, 1, high, jnp.minimum(h + 1, LOCAL_HEADS - 1))

        high = None
        for j in range(parts):
            high = score(0, 0, j, high)
        lax.fori_loop(0, LOCAL_HEADS, both_tiles, high)
        if e > 0:
            for j in range(4):
                send(("o", 4 - e, j), part.at[e, j], ret.at[(4 - e) - 1, j], at_z(e))
                send(("l", 4 - e, j), stat.at[e, j], rstat.at[(4 - e) - 1, j], at_z(e))

    for e in (3, 2, 1, 0):
        if e > 0:
            for j in range(4):
                arrive(("qz", e, j))
        attend(e)
        if e == 3:
            for j in range(4):
                if j > 0:
                    arrive(("s", j))
                for h in range(LOCAL_HEADS):
                    skt[j, h] = sx[j, 0, pl.ds(h * HEAD, HEAD), :].T
            for d in range(3):
                for j in range(4):
                    slot = (j + 4 - (z + d) // 4) % 4
                    half = pl.ds((j % 2) * ROWS, ROWS)
                    for h in range(LOCAL_HEADS):
                        kloc[d, j // 2, h, half, :] = skt[slot, h]
                    vloc[d, j // 2, :, half] = sx[slot, 1]

    for j in (2, 1, 3, 0):
        for b in (1, 2, 3):
            arrive(("o", b, j))
            arrive(("l", b, j))
        lses = [stat[0, j]] + [rstat[b, j] for b in range(3)]
        top = functools.reduce(jnp.maximum, lses)
        weights = [jnp.exp(v - top) for v in lses]
        inverse = 1.0 / sum(weights[1:], weights[0])
        coefs = [w * inverse for w in weights]
        for h in range(LOCAL_HEADS):
            rows = pl.ds(h * HEAD, HEAD)
            acc = coefs[0][h : h + 1, :] * part[0, j, rows, :].astype(F32)
            for b in range(3):
                acc += coefs[b + 1][h : h + 1, :] * ret[b, j, rows, :].astype(F32)
            merged[j, rows, :] = acc.astype(BF16)
        if j > 0:
            send(("a", 4 - j), merged.at[j], att.at[4 - j], at_x(j))
    mix_t[own, :] = merged[0]
    for j in (2, 1, 3):
        arrive(("a", j))
        mix_t[pl.ds(pl.multiple_of(((x + j) % 4) * HROWS, HROWS), HROWS), :] = att[j]

    loads[3].wait()
    mix = jnp.concatenate([mix_t[pl.ds(b * 128, 128), :].T for b in range(10)], axis=1)
    attended = unit(jnp.dot(mix, wout[...], preferred_element_type=F32))
    hidden = hid[...]
    hidden = unit(hidden + arate_ref[...] * (attended - hidden))
    hid[...] = hidden
    upper, lower = pl.ds(0, ROWS), pl.ds(ROWS, ROWS)
    blocks[0, upper, :] = hidden.astype(BF16)

    halves = (pl.ds(0, 64), pl.ds(64, 64))
    mirror = (pl.ds(ROWS, 64), pl.ds(ROWS + 64, 64))
    send(("b", 3), blocks.at[0, upper], blocks.at[3, upper], at_y(1))
    send(("b", 1), blocks.at[0, upper], blocks.at[1, upper], at_y(3))
    send(("p", 0), blocks.at[0, upper], blocks.at[0, lower], partner)

    def swiglu(i):
        a = blocks[i]
        up = jnp.dot(a, wup[...], preferred_element_type=F32) * uscale_ref[...]
        gate = jnp.dot(a, wgate[...], preferred_element_type=F32) * (gscale_ref[...] * math.sqrt(D))
        act = (up * (gate / (1.0 + jnp.exp(-gate)))).astype(BF16)
        both = jnp.dot(act, wdown[...], preferred_element_type=F32)
        give[i] = both[ROWS:].astype(BF16)
        total[i] = both[:ROWS]
        send(("x", i), give.at[i], take.at[i], partner)

    def join(i):
        arrive(("x", i))
        both = total[i] + take[i].astype(F32)
        if i == 0:
            total[0] = both
        else:
            send_y[i - 1] = both.astype(BF16)
            send(("y", 4 - i), send_y.at[i - 1], recv_y.at[3 - i], at_y(i))

    for n in (4, 5, 6):
        loads[n].wait()
    arrive(("p", 0))
    swiglu(0)
    arrive(("b", 3))
    send(("f", 0), blocks.at[3, halves[0]], blocks.at[2, halves[0]], at_y(1))
    send(("p", 3), blocks.at[3, upper], blocks.at[3, lower], partner)
    arrive(("b", 1))
    send(("f", 1), blocks.at[1, halves[1]], blocks.at[2, halves[1]], at_y(3))
    send(("p", 1), blocks.at[1, upper], blocks.at[1, lower], partner)
    arrive(("p", 3))
    swiglu(3)
    for k in (0, 1):
        arrive(("f", k))
        send(("g", k), blocks.at[2, halves[k]], blocks.at[2, mirror[k]], partner)
    arrive(("p", 1))
    join(3)
    swiglu(1)
    for k in (0, 1):
        arrive(("g", k))
    join(1)
    swiglu(2)
    join(2)
    join(0)
    summed = total[0]
    for i in (1, 3, 2):
        arrive(("y", i))
        summed += recv_y[i - 1].astype(F32)
    hidden = hid[...]
    hidden = unit(hidden + mrate_ref[...] * (unit(summed) - hidden))
    out_ref[...] = (math.sqrt(D) * hidden).astype(BF16)
    for copy in sends:
        copy.wait_send()


def body(
    tokens, seg_lengths, prefix_keys, prefix_values, w_qkv, w_out, qk_scale, attn_rate,
    w_up, w_gate, w_down, up_scale, gate_scale, mlp_rate,
):
    vmem = pl.BlockSpec(memory_space=pltpu.VMEM)
    smem = pl.BlockSpec(memory_space=pltpu.SMEM)
    hbm = pl.BlockSpec(memory_space=pltpu.HBM)
    ff = w_up.shape[1]
    vm = pltpu.VMEM
    out = pl.pallas_call(
        layer_kernel,
        out_shape=jax.ShapeDtypeStruct((ROWS, D), BF16),
        in_specs=[smem, vmem, vmem, vmem, hbm, hbm, vmem, vmem, hbm, hbm, hbm, vmem, vmem, vmem],
        out_specs=vmem,
        scratch_shapes=[
            vm((D, 3 * D), BF16), vm((D, D), BF16), vm((D, ff), BF16), vm((D, ff), BF16), vm((ff, D), BF16),
            vm((D, 128), F32),
            vm((D, PREF), BF16), vm((D, PREF), BF16), vm((D, ROWS), BF16), vm((2, D, ROWS), BF16),
            vm((4, HROWS, PREF), BF16), vm((4, HROWS, PREF), BF16), vm((4, HROWS, ROWS), BF16),
            vm((4, 2, HROWS, ROWS), BF16), vm((3, 4, HROWS, ROWS), BF16),
            vm((LOCAL_HEADS, 4 * PREF, HEAD), BF16), vm((4, LOCAL_HEADS, ROWS, HEAD), BF16),
            vm((16, 8, ROWS), jnp.int32), vm((3, 2, PREF, PREF), F32), vm((2, 5 * PREF, 2 * ROWS), F32),
            vm((3, 2, LOCAL_HEADS, PREF, HEAD), BF16), vm((3, 2, HROWS, PREF), BF16),
            vm((4, 4, HROWS, ROWS), BF16), vm((4, 4, 8, ROWS), F32),
            vm((3, 4, HROWS, ROWS), BF16), vm((3, 4, 8, ROWS), F32),
            vm((4, HROWS, ROWS), BF16), vm((4, HROWS, ROWS), BF16), vm((D, ROWS), BF16),
            vm((ROWS, D), F32), vm((4, 2 * ROWS, D), BF16), vm((4, ROWS, D), BF16), vm((4, ROWS, D), BF16),
            vm((4, ROWS, D), F32), vm((3, ROWS, D), BF16), vm((3, ROWS, D), BF16),
            pltpu.SemaphoreType.DMA((7,)), pltpu.SemaphoreType.DMA((140,)),
        ],
        compiler_params=pltpu.CompilerParams(
            collective_id=0, has_side_effects=True, vmem_limit_bytes=56 * 1024 * 1024
        ),
        name="layer",
    )(
        seg_lengths, tokens[0], prefix_keys[0], prefix_values[0], w_qkv, w_out, qk_scale.reshape(1, D),
        attn_rate.reshape(1, D), w_up, w_gate, w_down, up_scale.reshape(1, ff), gate_scale.reshape(1, ff),
        mlp_rate.reshape(1, D),
    )
    return out[None]


def solution(mesh):
    in_specs = (
        P("grp", "tok", None), P("grp", None), P("grp", "tok", None), P("grp", "tok", None),
        P(), P(), P(), P(), P(None, "grp"), P(None, "grp"), P("grp", None), P("grp"), P("grp"), P(),
    )
    return jax.shard_map(body, mesh=mesh, in_specs=in_specs, out_specs=P("grp", "tok", None), check_vma=False)
```

profile of v0, /device:TPU:1, one launch (start us, length us, event | category | flops | bytes accessed | tf_op | source)
XLA Modules:
  0.0 106.3 jit_solution(7509836868124747266)
XLA Ops:
  0.0 1.3 %reshape.17.uscale_ref = f32[1,640]{1,0:T(1,128)} reshape(f32[640]{0:T(1024)} %param.25) | data formatting | bytes 5120 | tf_op jit(solution)/shard_map/reshape | solution.py:402
  1.3 1.3 %reshape.18.gscale_ref = f32[1,640]{1,0:T(1,128)} reshape(f32[640]{0:T(1024)} %param.26) | data formatting | bytes 5120 | tf_op jit(solution)/shard_map/reshape | solution.py:402
  2.5 1.3 %reshape.15.scale_ref = f32[1,1280]{1,0:T(1,128)} reshape(f32[1280]{0:T(1024)} %param.20) | data formatting | bytes 10240 | tf_op jit(solution)/shard_map/reshape | solution.py:401
  3.8 1.3 %reshape.16.arate_ref = f32[1,1280]{1,0:T(1,128)} reshape(f32[1280]{0:T(1024)} %param.21) | data formatting | bytes 10240 | tf_op jit(solution)/shard_map/reshape | solution.py:402
  5.1 1.3 %reshape.19.mrate_ref = f32[1,1280]{1,0:T(1,128)} reshape(f32[1280]{0:T(1024)} %param.27) | data formatting | bytes 10240 | tf_op jit(solution)/shard_map/reshape | solution.py:403
  6.4 98.1 %layer.1 = bf16[128,1280]{1,0:T(8,128)(2,1)} custom-call(s32[1,32]{1,0:T(1,128)} %lengths_ref.1, bf16[128,1280]{1,0:T(8,128)(2,1)} %bitcast.7, bf16[256,1280]{1,0:T(8,128)(2,1)} %bitcast.5, bf16[256,1280]{1,0:T(8,128)(2,1)} %bitcast.6, bf16[1280,3840]{1,0:T(8,128)(2,1)} %wqkv_hbm.1, bf16[1280,1280]{1,0:T(8,128)(2,1)} %wout_hbm.1, ...), custom_call_target="tpu_custom_call" | custom-call | tf_op jit(solution)/shard_map/layer/pallas_call | solution.py:375
  104.5 1.7 %copy.16 = bf16[1,128,1280]{2,1,0:T(8,128)(2,1)} copy(bf16[1,128,1280]{2,1,0:T(8,128)(2,1)} %bitcast.4) | data formatting | bytes 655360
where the time goes:
time: 107 us; the launch traced here: 106 us
  Pallas kernels  98.1 us (92%)
  local copies, waits for them, and re-layouts  8.13 us (8%)
    pallas_call x1, Pallas kernels, body(): pl.pallas_call(layer_kernel, out_shape=jax.ShapeDtypeStruct((ROWS, D), BF...  98.1 us

commit v1 on v0

--- a/solution.py
+++ b/solution.py
@@ -32,10 +32,10 @@
 
 
 def layer_kernel(
-    lengths_ref, tok_ref, pk_ref, pv_ref, wqkv_hbm, wout_hbm, scale_ref, arate_ref, wup_hbm, wgate_hbm, wdown_hbm,
+    lengths_ref, tok_hbm, pk_hbm, pv_hbm, wqkv_hbm, wout_hbm, scale_ref, arate_ref, wup_hbm, wgate_hbm, wdown_hbm,
     uscale_ref, gscale_ref, mrate_ref, out_ref,
-    wqkv, wout, wup, wgate, wdown, scale_t,
-    key_s, val_s, q_s, sk_s, kx, vx, qx, sx, qz, kt, skt, starts, mask, sbuf, kloc, vloc, part, stat, ret, rstat, merged, att, mix_t,
+    tok_ref, pk_ref, pv_ref, wqkv, wout, wup, wgate, wdown, scale_t,
+    key_s, val_s, q_s, sk_s, kx, vx, qx, sx, qz, kt, skt, starts, mask, sbuf, kloc, vloc, held, tops, sums, part, stat, ret, rstat, merged, att, mix_t,
     hid, blocks, give, take, total, send_y, recv_y, w_sem, sem,
 ):
     tok, grp = lax.axis_index("tok"), lax.axis_index("grp")
@@ -74,30 +74,33 @@
             device_id_type=MESH,
         ).wait_recv()
 
+    loads = {}
+
+    def load(name, src, dst):
+        copy = pltpu.make_async_copy(src, dst, w_sem.at[len(loads)])
+        copy.start()
+        loads[name] = copy
+
+    load("pk", pk_hbm, pk_ref)
+    load("tok", tok_hbm, tok_ref)
+    load("pv", pv_hbm, pv_ref)
     barrier = pltpu.get_barrier_semaphore()
     for i in (1, 2, 3):
         for dev in (at_x(i), at_z(i), at_y(i)):
             pl.semaphore_signal(barrier, inc=1, device_id=dev, device_id_type=MESH)
     pl.semaphore_signal(barrier, inc=1, device_id=partner, device_id_type=MESH)
-
-    loads = []
-
-    def load(src, dst):
-        copy = pltpu.make_async_copy(src, dst, w_sem.at[len(loads)])
-        copy.start()
-        loads.append(copy)
-
     for n in range(3):
         cols = pl.ds(n * D, D)
-        load(wqkv_hbm.at[:, cols], wqkv.at[:, cols])
-    load(wout_hbm, wout)
-    load(wup_hbm, wup)
-    load(wgate_hbm, wgate)
-    load(wdown_hbm, wdown)
+        load(n, wqkv_hbm.at[:, cols], wqkv.at[:, cols])
+    load("out", wout_hbm, wout)
+    load("up", wup_hbm, wup)
+    load("gate", wgate_hbm, wgate)
+    load("down", wdown_hbm, wdown)
 
     for b in range(10):
         lanes = pl.ds(b * 128, 128)
-        scale_t[lanes, :] = jnp.broadcast_to(scale_ref[:, lanes], (128, 128)).T
+        scale_t[lanes, :] = jnp.broadcast_to(scale_ref[lanes].reshape(1, 128), (128, 128)).T
+    loads["pk"].wait()
     for b in range(10):
         lanes = pl.ds(b * 128, 128)
         scale = scale_t[lanes, :]
@@ -108,13 +111,15 @@
     def rows_of(ref, i):
         return ref.at[pl.ds(((x + i) % 4) * HROWS, HROWS), :]
 
-    for i in (2, 1, 3):
+    for i in (1, 3):
         send(("k", 4 - i), rows_of(key_s, i), kx.at[4 - i], at_x(i))
 
+    loads["pv"].wait()
     for b in range(10):
         lanes = pl.ds(b * 128, 128)
         val_s[lanes, :] = pv_ref[:, lanes].T
 
+    loads["tok"].wait()
     hidden = unit(tok_ref[...].astype(F32))
     hid[...] = hidden
     hidden = hidden.astype(BF16)
@@ -138,8 +143,10 @@
             send(("qz", 4 - e, j), qx.at[j], qz.at[(4 - e) - 1, j], at_z(e))
 
     forward_q(0)
-    for i in (2, 1, 3):
+    for i in (1, 3):
         send(("v", 4 - i), rows_of(val_s, i), vx.at[4 - i], at_x(i))
+    send(("k", 2), rows_of(key_s, 2), kx.at[2], at_x(2))
+    send(("v", 2), rows_of(val_s, 2), vx.at[2], at_x(2))
     for n in (1, 2):
         loads[n].wait()
         for b in range(5):
@@ -186,21 +193,19 @@
             kt[h, pl.ds(j * PREF, PREF), :] = kx[j, pl.ds(h * HEAD, HEAD), :].T
 
     turn_keys(0)
-    for j in (1, 3, 2):
+    for j in (1, 3):
         arrive(("k", j))
         turn_keys(j)
     for j in (1, 3, 2):
         arrive(("q", j))
         forward_q(j)
-    for j in (1, 3, 2):
+    for j in (1, 3):
         arrive(("v", j))
 
     def fold(v):
         return v.reshape(v.shape[0] // 8, 8, v.shape[1])
 
-    def attend(e):
-        local = e < 3
-
+    def attend(e, parts, last):
         def head_rows(h):
             return pl.ds(pl.multiple_of(h * HEAD, HEAD), HEAD)
 
@@ -223,21 +228,30 @@
             t = jnp.dot(values, p.astype(BF16), preferred_element_type=F32)
             return (more, t) if o is None else (added + more, o + t)
 
-        parts = 5 if local else 4
-
         def step(h, n, high, after):
             m = jnp.max(high, axis=0, keepdims=True)
             high, added, o = None, None, None
-            for j in range(parts):
+            for j in parts:
                 high = score(after, 1 - n, j, high)
                 added, o = blend(h, n, j, m, added, o)
             added = jnp.sum(added, axis=0, keepdims=True)
-            o = (o * (1.0 / added)).astype(BF16)
-            lse = m + jnp.log(added)
+            rows, row = head_rows(h), pl.ds(h, 1)
+            halves = (slice(0, ROWS), slice(ROWS, 2 * ROWS))
+            if not last:
+                held[e, n, rows, :] = o
+                tops[e, n, row, :] = m
+                sums[e, n, row, :] = added
+                return high
+            m_old = tops[e, n, row, :]
+            m_new = jnp.maximum(m, m_old)
+            grow, keep = jnp.exp(m - m_new), jnp.exp(m_old - m_new)
+            added = grow * added + keep * sums[e, n, row, :]
+            inverse = 1.0 / added
+            o = ((grow * inverse) * o + (keep * inverse) * held[e, n, rows, :]).astype(BF16)
+            lse = m_new + jnp.log(added)
             for a in (0, 1):
-                lanes = slice(a * ROWS, (a + 1) * ROWS)
-                part[e, 2 * n + a, head_rows(h), :] = o[:, lanes]
-                stat[e, 2 * n + a, pl.ds(h, 1), :] = lse[:, lanes]
+                part[e, 2 * n + a, rows, :] = o[:, halves[a]]
+                stat[e, 2 * n + a, row, :] = lse[:, halves[a]]
             return high
 
         def both_tiles(h, high):
@@ -245,32 +259,37 @@
             return step(h, 1, high, jnp.minimum(h + 1, LOCAL_HEADS - 1))
 
         high = None
-        for j in range(parts):
+        for j in parts:
             high = score(0, 0, j, high)
         lax.fori_loop(0, LOCAL_HEADS, both_tiles, high)
-        if e > 0:
+        if last and e > 0:
             for j in range(4):
                 send(("o", 4 - e, j), part.at[e, j], ret.at[(4 - e) - 1, j], at_z(e))
                 send(("l", 4 - e, j), stat.at[e, j], rstat.at[(4 - e) - 1, j], at_z(e))
 
-    for e in (3, 2, 1, 0):
+    for e in (0, 1, 3, 2):
         if e > 0:
             for j in range(4):
                 arrive(("qz", e, j))
-        attend(e)
-        if e == 3:
-            for j in range(4):
-                if j > 0:
-                    arrive(("s", j))
-                for h in range(LOCAL_HEADS):
-                    skt[j, h] = sx[j, 0, pl.ds(h * HEAD, HEAD), :].T
-            for d in range(3):
-                for j in range(4):
-                    slot = (j + 4 - (z + d) // 4) % 4
-                    half = pl.ds((j % 2) * ROWS, ROWS)
-                    for h in range(LOCAL_HEADS):
-                        kloc[d, j // 2, h, half, :] = skt[slot, h]
-                    vloc[d, j // 2, :, half] = sx[slot, 1]
+        attend(e, (0, 1, 3), False)
+    arrive(("k", 2))
+    turn_keys(2)
+    arrive(("v", 2))
+    attend(3, (2,), True)
+    for j in range(4):
+        if j > 0:
+            arrive(("s", j))
+        for h in range(LOCAL_HEADS):
+            skt[j, h] = sx[j, 0, pl.ds(h * HEAD, HEAD), :].T
+    for d in range(3):
+        for j in range(4):
+            slot = (j + 4 - (z + d) // 4) % 4
+            half = pl.ds((j % 2) * ROWS, ROWS)
+            for h in range(LOCAL_HEADS):
+                kloc[d, j // 2, h, half, :] = skt[slot, h]
+            vloc[d, j // 2, :, half] = sx[slot, 1]
+    for e in (2, 1, 0):
+        attend(e, (2, 4), True)
 
     for j in (2, 1, 3, 0):
         for b in (1, 2, 3):
@@ -294,11 +313,11 @@
         arrive(("a", j))
         mix_t[pl.ds(pl.multiple_of(((x + j) % 4) * HROWS, HROWS), HROWS), :] = att[j]
 
-    loads[3].wait()
+    loads["out"].wait()
     mix = jnp.concatenate([mix_t[pl.ds(b * 128, 128), :].T for b in range(10)], axis=1)
     attended = unit(jnp.dot(mix, wout[...], preferred_element_type=F32))
     hidden = hid[...]
-    hidden = unit(hidden + arate_ref[...] * (attended - hidden))
+    hidden = unit(hidden + arate_ref[...].reshape(1, D) * (attended - hidden))
     hid[...] = hidden
     upper, lower = pl.ds(0, ROWS), pl.ds(ROWS, ROWS)
     blocks[0, upper, :] = hidden.astype(BF16)
@@ -311,8 +330,8 @@
 
     def swiglu(i):
         a = blocks[i]
-        up = jnp.dot(a, wup[...], preferred_element_type=F32) * uscale_ref[...]
-        gate = jnp.dot(a, wgate[...], preferred_element_type=F32) * (gscale_ref[...] * math.sqrt(D))
+        up = jnp.dot(a, wup[...], preferred_element_type=F32) * uscale_ref[...].reshape(1, -1)
+        gate = jnp.dot(a, wgate[...], preferred_element_type=F32) * (gscale_ref[...].reshape(1, -1) * math.sqrt(D))
         act = (up * (gate / (1.0 + jnp.exp(-gate)))).astype(BF16)
         both = jnp.dot(act, wdown[...], preferred_element_type=F32)
         give[i] = both[ROWS:].astype(BF16)
@@ -328,7 +347,7 @@
             send_y[i - 1] = both.astype(BF16)
             send(("y", 4 - i), send_y.at[i - 1], recv_y.at[3 - i], at_y(i))
 
-    for n in (4, 5, 6):
+    for n in ("up", "gate", "down"):
         loads[n].wait()
     arrive(("p", 0))
     swiglu(0)
@@ -357,7 +376,7 @@
         arrive(("y", i))
         summed += recv_y[i - 1].astype(F32)
     hidden = hid[...]
-    hidden = unit(hidden + mrate_ref[...] * (unit(summed) - hidden))
+    hidden = unit(hidden + mrate_ref[...].reshape(1, D) * (unit(summed) - hidden))
     out_ref[...] = (math.sqrt(D) * hidden).astype(BF16)
     for copy in sends:
         copy.wait_send()
@@ -375,9 +394,10 @@
     out = pl.pallas_call(
         layer_kernel,
         out_shape=jax.ShapeDtypeStruct((ROWS, D), BF16),
-        in_specs=[smem, vmem, vmem, vmem, hbm, hbm, vmem, vmem, hbm, hbm, hbm, vmem, vmem, vmem],
+        in_specs=[smem, hbm, hbm, hbm, hbm, hbm, vmem, vmem, hbm, hbm, hbm, vmem, vmem, vmem],
         out_specs=vmem,
         scratch_shapes=[
+            vm((ROWS, D), BF16), vm((PREF, D), BF16), vm((PREF, D), BF16),
             vm((D, 3 * D), BF16), vm((D, D), BF16), vm((D, ff), BF16), vm((D, ff), BF16), vm((ff, D), BF16),
             vm((D, 128), F32),
             vm((D, PREF), BF16), vm((D, PREF), BF16), vm((D, ROWS), BF16), vm((2, D, ROWS), BF16),
@@ -386,21 +406,21 @@
             vm((LOCAL_HEADS, 4 * PREF, HEAD), BF16), vm((4, LOCAL_HEADS, ROWS, HEAD), BF16),
             vm((16, 8, ROWS), jnp.int32), vm((3, 2, PREF, PREF), F32), vm((2, 5 * PREF, 2 * ROWS), F32),
             vm((3, 2, LOCAL_HEADS, PREF, HEAD), BF16), vm((3, 2, HROWS, PREF), BF16),
+            vm((4, 2, HROWS, PREF), F32), vm((4, 2, 8, PREF), F32), vm((4, 2, 8, PREF), F32),
             vm((4, 4, HROWS, ROWS), BF16), vm((4, 4, 8, ROWS), F32),
             vm((3, 4, HROWS, ROWS), BF16), vm((3, 4, 8, ROWS), F32),
             vm((4, HROWS, ROWS), BF16), vm((4, HROWS, ROWS), BF16), vm((D, ROWS), BF16),
             vm((ROWS, D), F32), vm((4, 2 * ROWS, D), BF16), vm((4, ROWS, D), BF16), vm((4, ROWS, D), BF16),
             vm((4, ROWS, D), F32), vm((3, ROWS, D), BF16), vm((3, ROWS, D), BF16),
-            pltpu.SemaphoreType.DMA((7,)), pltpu.SemaphoreType.DMA((140,)),
+            pltpu.SemaphoreType.DMA((10,)), pltpu.SemaphoreType.DMA((140,)),
         ],
         compiler_params=pltpu.CompilerParams(
             collective_id=0, has_side_effects=True, vmem_limit_bytes=56 * 1024 * 1024
         ),
         name="layer",
     )(
-        seg_lengths, tokens[0], prefix_keys[0], prefix_values[0], w_qkv, w_out, qk_scale.reshape(1, D),
-        attn_rate.reshape(1, D), w_up, w_gate, w_down, up_scale.reshape(1, ff), gate_scale.reshape(1, ff),
-        mlp_rate.reshape(1, D),
+        seg_lengths, tokens[0], prefix_keys[0], prefix_values[0], w_qkv, w_out, qk_scale, attn_rate,
+        w_up, w_gate, w_down, up_scale, gate_scale, mlp_rate,
     )
     return out[None]
 

time: 107 us -> 101 us (0.944)
  local copies, waits for them, and re-layouts: 8.13 us -> 1.72 us
  Pallas kernels: 98.1 us -> 99.5 us
    reshape x5 -> x0, local copies, waits for them, and re-layouts: 6.41 us -> none  [the longest x1 1.29 us: body(): qk_scale.reshape(1, D)]
    pallas_call x1, Pallas kernels: 98.1 us -> 99.5 us  [body(): pl.pallas_call(layer_kernel, out_shape=jax.ShapeDtypeStruct((ROWS, D), BF...]
where the time goes in v1:
time: 101 us
  Pallas kernels  99.5 us (99%)
  local copies, waits for them, and re-layouts  1.72 us (2%)
    pallas_call x1, Pallas kernels, body(): pl.pallas_call(layer_kernel, out_shape=jax.ShapeDtypeStruct((ROWS, D), BF...  99.5 us

profile of v1, /device:TPU:1, one launch (start us, length us, event | category | flops | bytes accessed | tf_op | source)
XLA Modules:
  0.0 101.3 jit_solution(4539775253595968696)
XLA Ops:
  0.0 99.5 %layer.1 = bf16[128,1280]{1,0:T(8,128)(2,1)} custom-call(s32[1,32]{1,0:T(1,128)} %lengths_ref.1, bf16[128,1280]{1,0:T(8,128)(2,1)} %bitcast.7, bf16[256,1280]{1,0:T(8,128)(2,1)} %bitcast.5, bf16[256,1280]{1,0:T(8,128)(2,1)} %bitcast.6, bf16[1280,3840]{1,0:T(8,128)(2,1)} %wqkv_hbm.1, bf16[1280,1280]{1,0:T(8,128)(2,1)} %wout_hbm.1, f32[1280]{0:T(1024)} %scale_ref.1, ...), custom_call_target="tpu_custom_call" | custom-call | tf_op jit(solution)/shard_map/layer/pallas_call | solution.py:394
  99.6 1.7 %copy.16 = bf16[1,128,1280]{2,1,0:T(8,128)(2,1)} copy(bf16[1,128,1280]{2,1,0:T(8,128)(2,1)} %bitcast.4) | data formatting | bytes 655360

commit v2 on v1

--- a/solution.py
+++ b/solution.py
@@ -139,14 +139,12 @@
     qx[0] = q_s[pl.ds(pl.multiple_of(x * HROWS, HROWS), HROWS), :]
 
     def forward_q(j):
-        for e in (2, 1, 3):
+        for e in (1, 3):
             send(("qz", 4 - e, j), qx.at[j], qz.at[(4 - e) - 1, j], at_z(e))
 
     forward_q(0)
     for i in (1, 3):
         send(("v", 4 - i), rows_of(val_s, i), vx.at[4 - i], at_x(i))
-    send(("k", 2), rows_of(key_s, 2), kx.at[2], at_x(2))
-    send(("v", 2), rows_of(val_s, 2), vx.at[2], at_x(2))
     for n in (1, 2):
         loads[n].wait()
         for b in range(5):
@@ -155,9 +153,6 @@
                 if n == 1:
                     cols = head_unit(cols, scale_t[lanes, :])
                 sk_s[n - 1, lanes, :] = cols.astype(BF16)
-    for i in (2, 1, 3):
-        src = sk_s.at[:, pl.ds(((x + i) % 4) * HROWS, HROWS), :]
-        send(("s", 4 - i), src, sx.at[4 - i], at_x(i))
     own = pl.ds(pl.multiple_of(x * HROWS, HROWS), HROWS)
     kx[0] = key_s[own, :]
     vx[0] = val_s[own, :]
@@ -201,6 +196,8 @@
         forward_q(j)
     for j in (1, 3):
         arrive(("v", j))
+    send(("k", 2), rows_of(key_s, 2), kx.at[2], at_x(2))
+    send(("v", 2), rows_of(val_s, 2), vx.at[2], at_x(2))
 
     def fold(v):
         return v.reshape(v.shape[0] // 8, 8, v.shape[1])
@@ -242,13 +239,17 @@
                 tops[e, n, row, :] = m
                 sums[e, n, row, :] = added
                 return high
-            m_old = tops[e, n, row, :]
-            m_new = jnp.maximum(m, m_old)
-            grow, keep = jnp.exp(m - m_new), jnp.exp(m_old - m_new)
-            added = grow * added + keep * sums[e, n, row, :]
-            inverse = 1.0 / added
-            o = ((grow * inverse) * o + (keep * inverse) * held[e, n, rows, :]).astype(BF16)
-            lse = m_new + jnp.log(added)
+            if e < 3:
+                m_old = tops[e, n, row, :]
+                m_new = jnp.maximum(m, m_old)
+                grow, keep = jnp.exp(m - m_new), jnp.exp(m_old - m_new)
+                added = grow * added + keep * sums[e, n, row, :]
+                inverse = 1.0 / added
+                o = ((grow * inverse) * o + (keep * inverse) * held[e, n, rows, :]).astype(BF16)
+                m = m_new
+            else:
+                o = (o * (1.0 / added)).astype(BF16)
+            lse = m + jnp.log(added)
             for a in (0, 1):
                 part[e, 2 * n + a, rows, :] = o[:, halves[a]]
                 stat[e, 2 * n + a, row, :] = lse[:, halves[a]]
@@ -263,19 +264,29 @@
             high = score(0, 0, j, high)
         lax.fori_loop(0, LOCAL_HEADS, both_tiles, high)
         if last and e > 0:
-            for j in range(4):
+            for j in (2, 1, 3, 0):
                 send(("o", 4 - e, j), part.at[e, j], ret.at[(4 - e) - 1, j], at_z(e))
                 send(("l", 4 - e, j), stat.at[e, j], rstat.at[(4 - e) - 1, j], at_z(e))
 
-    for e in (0, 1, 3, 2):
-        if e > 0:
-            for j in range(4):
-                arrive(("qz", e, j))
-        attend(e, (0, 1, 3), False)
+    def queries_here(e):
+        for j in range(4):
+            arrive(("qz", e, j))
+
+    attend(0, (0, 1, 3), False)
+    for j in (0, 1, 3, 2):
+        send(("qz", 2, j), qx.at[j], qz.at[1, j], at_z(2))
+    queries_here(1)
+    attend(1, (0, 1, 3), False)
+    for i in (2, 1, 3):
+        src = sk_s.at[:, pl.ds(((x + i) % 4) * HROWS, HROWS), :]
+        send(("s", 4 - i), src, sx.at[4 - i], at_x(i))
     arrive(("k", 2))
     turn_keys(2)
     arrive(("v", 2))
-    attend(3, (2,), True)
+    queries_here(3)
+    attend(3, (0, 1, 3, 2), True)
+    queries_here(2)
+    attend(2, (0, 1, 3), False)
     for j in range(4):
         if j > 0:
             arrive(("s", j))
@@ -288,7 +299,7 @@
             for h in range(LOCAL_HEADS):
                 kloc[d, j // 2, h, half, :] = skt[slot, h]
             vloc[d, j // 2, :, half] = sx[slot, 1]
-    for e in (2, 1, 0):
+    for e in (1, 2, 0):
         attend(e, (2, 4), True)
 
     for j in (2, 1, 3, 0):
@@ -323,57 +334,66 @@
     blocks[0, upper, :] = hidden.astype(BF16)
 
     halves = (pl.ds(0, 64), pl.ds(64, 64))
-    mirror = (pl.ds(ROWS, 64), pl.ds(ROWS + 64, 64))
-    send(("b", 3), blocks.at[0, upper], blocks.at[3, upper], at_y(1))
-    send(("b", 1), blocks.at[0, upper], blocks.at[1, upper], at_y(3))
+    ours, theirs = (pl.ds(0, 64), pl.ds(ROWS, 64)), (pl.ds(64, 64), pl.ds(ROWS + 64, 64))
+    for i, k in ((3, 0), (1, 1), (3, 1), (1, 0)):
+        send(("b", i, k), blocks.at[0, halves[k]], blocks.at[i, ours[k]], at_y(4 - i))
     send(("p", 0), blocks.at[0, upper], blocks.at[0, lower], partner)
 
-    def swiglu(i):
-        a = blocks[i]
+    def share(i, k):
+        send(("p", i, k), blocks.at[i, ours[k]], blocks.at[i, theirs[k]], partner)
+
+    def swiglu(i, rows):
+        size = rows.size // 2
+        mine = pl.ds(rows.start // 2, size)
+        a = blocks[i, rows, :]
         up = jnp.dot(a, wup[...], preferred_element_type=F32) * uscale_ref[...].reshape(1, -1)
         gate = jnp.dot(a, wgate[...], preferred_element_type=F32) * (gscale_ref[...].reshape(1, -1) * math.sqrt(D))
         act = (up * (gate / (1.0 + jnp.exp(-gate)))).astype(BF16)
         both = jnp.dot(act, wdown[...], preferred_element_type=F32)
-        give[i] = both[ROWS:].astype(BF16)
-        total[i] = both[:ROWS]
-        send(("x", i), give.at[i], take.at[i], partner)
-
-    def join(i):
-        arrive(("x", i))
-        both = total[i] + take[i].astype(F32)
+        give[i, mine, :] = both[size:].astype(BF16)
+        total[i, mine, :] = both[:size]
+        send(("x", i, rows.start), give.at[i, mine], take.at[i, mine], partner)
+
+    def join(i, rows):
+        mine = pl.ds(rows.start // 2, rows.size // 2)
+        arrive(("x", i, rows.start))
+        both = total[i, mine, :] + take[i, mine, :].astype(F32)
         if i == 0:
             total[0] = both
         else:
-            send_y[i - 1] = both.astype(BF16)
-            send(("y", 4 - i), send_y.at[i - 1], recv_y.at[3 - i], at_y(i))
-
+            send_y[i - 1, mine, :] = both.astype(BF16)
+            send(("y", 4 - i, rows.start), send_y.at[i - 1, mine], recv_y.at[3 - i, mine], at_y(i))
+
+    whole, parts = pl.ds(0, 2 * ROWS), (pl.ds(0, ROWS), pl.ds(ROWS, ROWS))
     for n in ("up", "gate", "down"):
         loads[n].wait()
     arrive(("p", 0))
-    swiglu(0)
-    arrive(("b", 3))
-    send(("f", 0), blocks.at[3, halves[0]], blocks.at[2, halves[0]], at_y(1))
-    send(("p", 3), blocks.at[3, upper], blocks.at[3, lower], partner)
-    arrive(("b", 1))
-    send(("f", 1), blocks.at[1, halves[1]], blocks.at[2, halves[1]], at_y(3))
-    send(("p", 1), blocks.at[1, upper], blocks.at[1, lower], partner)
-    arrive(("p", 3))
-    swiglu(3)
-    for k in (0, 1):
-        arrive(("f", k))
-        send(("g", k), blocks.at[2, halves[k]], blocks.at[2, mirror[k]], partner)
-    arrive(("p", 1))
-    join(3)
-    swiglu(1)
-    for k in (0, 1):
-        arrive(("g", k))
-    join(1)
-    swiglu(2)
-    join(2)
-    join(0)
+    swiglu(0, whole)
+    for i, k in ((3, 0), (1, 1)):
+        arrive(("b", i, k))
+        send(("b", 2, k), blocks.at[i, ours[k]], blocks.at[2, ours[k]], at_y(4 - i))
+        share(i, k)
+    held_back = None
+    for i, k in ((3, 0), (1, 1), (3, 1), (1, 0), (2, 0), (2, 1)):
+        if (i, k) == (1, 1):
+            for pair in ((3, 1), (1, 0)):
+                arrive(("b",) + pair)
+                share(*pair)
+        if (i, k) == (1, 0):
+            for pair in ((2, 0), (2, 1)):
+                arrive(("b",) + pair)
+                share(*pair)
+        arrive(("p", i, k))
+        swiglu(i, parts[k])
+        if held_back is not None:
+            join(*held_back)
+        held_back = (i, parts[k])
+    join(*held_back)
+    join(0, whole)
     summed = total[0]
     for i in (1, 3, 2):
-        arrive(("y", i))
+        arrive(("y", i, 0))
+        arrive(("y", i, ROWS))
         summed += recv_y[i - 1].astype(F32)
     hidden = hid[...]
     hidden = unit(hidden + mrate_ref[...].reshape(1, D) * (unit(summed) - hidden))
@@ -406,13 +426,13 @@
             vm((LOCAL_HEADS, 4 * PREF, HEAD), BF16), vm((4, LOCAL_HEADS, ROWS, HEAD), BF16),
             vm((16, 8, ROWS), jnp.int32), vm((3, 2, PREF, PREF), F32), vm((2, 5 * PREF, 2 * ROWS), F32),
             vm((3, 2, LOCAL_HEADS, PREF, HEAD), BF16), vm((3, 2, HROWS, PREF), BF16),
-            vm((4, 2, HROWS, PREF), F32), vm((4, 2, 8, PREF), F32), vm((4, 2, 8, PREF), F32),
+            vm((3, 2, HROWS, PREF), F32), vm((3, 2, 8, PREF), F32), vm((3, 2, 8, PREF), F32),
             vm((4, 4, HROWS, ROWS), BF16), vm((4, 4, 8, ROWS), F32),
             vm((3, 4, HROWS, ROWS), BF16), vm((3, 4, 8, ROWS), F32),
             vm((4, HROWS, ROWS), BF16), vm((4, HROWS, ROWS), BF16), vm((D, ROWS), BF16),
             vm((ROWS, D), F32), vm((4, 2 * ROWS, D), BF16), vm((4, ROWS, D), BF16), vm((4, ROWS, D), BF16),
             vm((4, ROWS, D), F32), vm((3, ROWS, D), BF16), vm((3, ROWS, D), BF16),
-            pltpu.SemaphoreType.DMA((10,)), pltpu.SemaphoreType.DMA((140,)),
+            pltpu.SemaphoreType.DMA((10,)), pltpu.SemaphoreType.DMA((168,)),
         ],
         compiler_params=pltpu.CompilerParams(
             collective_id=0, has_side_effects=True, vmem_limit_bytes=56 * 1024 * 1024

time: 101 us -> 91.6 us (0.907)
  Pallas kernels: 99.5 us -> 89.7 us
    pallas_call x1, Pallas kernels: 99.5 us -> 89.7 us  [body(): pl.pallas_call(layer_kernel, out_shape=jax.ShapeDtypeStruct((ROWS, D), BF...]
where the time goes in v2:
time: 91.6 us; the launch traced here: 91.5 us
  Pallas kernels  89.7 us (98%)
  local copies, waits for them, and re-layouts  1.72 us (2%)
    pallas_call x1, Pallas kernels, body(): pl.pallas_call(layer_kernel, out_shape=jax.ShapeDtypeStruct((ROWS, D), BF...  89.7 us

profile of v2, /device:TPU:1, one launch (start us, length us, event | category | flops | bytes accessed | tf_op | source)
XLA Modules:
  0.0 91.5 jit_solution(12294219687104034160)
XLA Ops:
  0.0 89.7 %layer.1 = bf16[128,1280]{1,0:T(8,128)(2,1)} custom-call(s32[1,32]{1,0:T(1,128)} %lengths_ref.1, bf16[128,1280]{1,0:T(8,128)(2,1)} %bitcast.7, bf16[256,1280]{1,0:T(8,128)(2,1)} %bitcast.5, bf16[256,1280]{1,0:T(8,128)(2,1)} %bitcast.6, bf16[1280,3840]{1,0:T(8,128)(2,1)} %wqkv_hbm.1, bf16[1280,1280]{1,0:T(8,128)(2,1)} %wout_hbm.1, f32[1280]{0:T(1024)} %scale_ref.1, ...), custom_call_target="tpu_custom_call" | custom-call | tf_op jit(solution)/shard_map/layer/pallas_call | solution.py:414
  89.7 1.7 %copy.16 = bf16[1,128,1280]{2,1,0:T(8,128)(2,1)} copy(bf16[1,128,1280]{2,1,0:T(8,128)(2,1)} %bitcast.4) | data formatting | bytes 655360

commit v3 on v2

--- a/solution.py
+++ b/solution.py
@@ -36,7 +36,7 @@
     uscale_ref, gscale_ref, mrate_ref, out_ref,
     tok_ref, pk_ref, pv_ref, wqkv, wout, wup, wgate, wdown, scale_t,
     key_s, val_s, q_s, sk_s, kx, vx, qx, sx, qz, kt, skt, starts, mask, sbuf, kloc, vloc, held, tops, sums, part, stat, ret, rstat, merged, att, mix_t,
-    hid, blocks, give, take, total, send_y, recv_y, w_sem, sem,
+    hid, blocks, give, take, total, send_y, recv_y, passing, w_sem, sem,
 ):
     tok, grp = lax.axis_index("tok"), lax.axis_index("grp")
     x, z = tok // 4, tok % 4
@@ -194,10 +194,11 @@
     for j in (1, 3, 2):
         arrive(("q", j))
         forward_q(j)
+    send(("k", 2), rows_of(key_s, 2), kx.at[2], at_x(2))
+    send(("v", 2), rows_of(val_s, 2), vx.at[2], at_x(2))
+
     for j in (1, 3):
         arrive(("v", j))
-    send(("k", 2), rows_of(key_s, 2), kx.at[2], at_x(2))
-    send(("v", 2), rows_of(val_s, 2), vx.at[2], at_x(2))
 
     def fold(v):
         return v.reshape(v.shape[0] // 8, 8, v.shape[1])
@@ -272,9 +273,9 @@
         for j in range(4):
             arrive(("qz", e, j))
 
-    attend(0, (0, 1, 3), False)
     for j in (0, 1, 3, 2):
         send(("qz", 2, j), qx.at[j], qz.at[1, j], at_z(2))
+    attend(0, (0, 1, 3), False)
     queries_here(1)
     attend(1, (0, 1, 3), False)
     for i in (2, 1, 3):
@@ -358,9 +359,16 @@
         mine = pl.ds(rows.start // 2, rows.size // 2)
         arrive(("x", i, rows.start))
         both = total[i, mine, :] + take[i, mine, :].astype(F32)
+        k = rows.start // ROWS
         if i == 0:
             total[0] = both
+        elif i == 2:
+            send_y[1, mine, :] = both.astype(BF16)
+            send(("m", k), send_y.at[1, mine], passing.at[k], at_y((1, 3)[k]))
         else:
+            if (i, k) in ((1, 0), (3, 1)):
+                arrive(("m", k))
+                both += passing[k].astype(F32)
             send_y[i - 1, mine, :] = both.astype(BF16)
             send(("y", 4 - i, rows.start), send_y.at[i - 1, mine], recv_y.at[3 - i, mine], at_y(i))
 
@@ -374,12 +382,12 @@
         send(("b", 2, k), blocks.at[i, ours[k]], blocks.at[2, ours[k]], at_y(4 - i))
         share(i, k)
     held_back = None
-    for i, k in ((3, 0), (1, 1), (3, 1), (1, 0), (2, 0), (2, 1)):
+    for i, k in ((3, 0), (1, 1), (2, 0), (2, 1), (1, 0), (3, 1)):
         if (i, k) == (1, 1):
             for pair in ((3, 1), (1, 0)):
                 arrive(("b",) + pair)
                 share(*pair)
-        if (i, k) == (1, 0):
+        if (i, k) == (2, 0):
             for pair in ((2, 0), (2, 1)):
                 arrive(("b",) + pair)
                 share(*pair)
@@ -391,7 +399,7 @@
     join(*held_back)
     join(0, whole)
     summed = total[0]
-    for i in (1, 3, 2):
+    for i in (1, 3):
         arrive(("y", i, 0))
         arrive(("y", i, ROWS))
         summed += recv_y[i - 1].astype(F32)
@@ -432,6 +440,7 @@
             vm((4, HROWS, ROWS), BF16), vm((4, HROWS, ROWS), BF16), vm((D, ROWS), BF16),
             vm((ROWS, D), F32), vm((4, 2 * ROWS, D), BF16), vm((4, ROWS, D), BF16), vm((4, ROWS, D), BF16),
             vm((4, ROWS, D), F32), vm((3, ROWS, D), BF16), vm((3, ROWS, D), BF16),
+            vm((2, ROWS // 2, D), BF16),
             pltpu.SemaphoreType.DMA((10,)), pltpu.SemaphoreType.DMA((168,)),
         ],
         compiler_params=pltpu.CompilerParams(

time: 91.6 us -> 89.8 us (0.980)
  Pallas kernels: 89.7 us -> 87.9 us
    pallas_call x1, Pallas kernels: 89.7 us -> 87.9 us  [body(): pl.pallas_call(layer_kernel, out_shape=jax.ShapeDtypeStruct((ROWS, D), BF...]
where the time goes in v3:
time: 89.8 us; the launch traced here: 89.6 us
  Pallas kernels  87.9 us (98%)
  local copies, waits for them, and re-layouts  1.72 us (2%)
    pallas_call x1, Pallas kernels, body(): pl.pallas_call(layer_kernel, out_shape=jax.ShapeDtypeStruct((ROWS, D), BF...  87.9 us

profile of v3, /device:TPU:1, one launch (start us, length us, event | category | flops | bytes accessed | tf_op | source)
XLA Modules:
  0.0 89.6 jit_solution(15502866830383794529)
XLA Ops:
  0.0 87.9 %layer.1 = bf16[128,1280]{1,0:T(8,128)(2,1)} custom-call(s32[1,32]{1,0:T(1,128)} %lengths_ref.1, bf16[128,1280]{1,0:T(8,128)(2,1)} %bitcast.7, bf16[256,1280]{1,0:T(8,128)(2,1)} %bitcast.5, bf16[256,1280]{1,0:T(8,128)(2,1)} %bitcast.6, bf16[1280,3840]{1,0:T(8,128)(2,1)} %wqkv_hbm.1, bf16[1280,1280]{1,0:T(8,128)(2,1)} %wout_hbm.1, f32[1280]{0:T(1024)} %scale_ref.1, ...), custom_call_target="tpu_custom_call" | custom-call | tf_op jit(solution)/shard_map/layer/pallas_call | solution.py:422
  87.9 1.7 %copy.16 = bf16[1,128,1280]{2,1,0:T(8,128)(2,1)} copy(bf16[1,128,1280]{2,1,0:T(8,128)(2,1)} %bitcast.4) | data formatting | bytes 655360
